TPU v7x, 32 devices: a whole 2x2x4 slice. The times are simulated.
32 devices in a mesh: dp: 4 (over z), seq: 8 (over y, x, core).
Axes of the slice: x: 2, y: 2, z: 4, core: 2. Of those that a mesh axis runs over, the one named last changes fastest.
Arguments:
- slide_tiles: bfloat16 [64, 256, 384], P(('dp', 'seq')), parts along dimension 0, may hold values from -6 to 6
- norm_gain: float32 [2, 384], replicated, may hold values from 0.1 to 1.9
- in_weight: bfloat16 [2, 384, 1536], replicated, may hold values from -0.3125 to 0.3125
- state_weight: bfloat16 [2, 384, 44], replicated, may hold values from -0.3125 to 0.3125
- conv_weight: float32 [2, 4, 800], replicated, may hold values from -2.5 to 2.5
- conv_bias: float32 [2, 800], replicated, may hold values from -0.5 to 0.5
- step_bias: float32 [2, 12], replicated, may hold values from -5 to -3
- decay_log: float32 [2, 12], replicated, may hold values from -8.5 to 1
- skip_gain: float32 [2, 12], replicated, may hold values from 0.5 to 1.5
- out_gain: float32 [2, 768], replicated, may hold values from 0.1 to 1.9
- out_weight: bfloat16 [2, 768, 384], replicated, may hold values from -0.21875 to 0.21875
Outputs:
- tile_out: bfloat16 [64, 256, 384], P(('dp', 'seq')), parts along dimension 0
There are 4 independent parts, one for each index of `dp`. A program takes and returns all parts, laid end to end along the dimension named above; an argument that names none is the same for every part. Nothing has to cross between parts.
All inputs are finite; a program needn't handle non-finite values.
Results may differ from a plain program's by a relative error of at most 0.014.
Values may be sent and summed in bfloat16 or wider, within the bound.
A program may use at most 64 MiB of HBM per device.

v0:
```python
import jax
import jax.numpy as jnp
from jax import lax
from jax.sharding import PartitionSpec as P

HEADS = 12
HEADDIM = 64
STATE = 16
GROUP = 256
epsilon = 1e-05


def entering_2(x, axis, join, neutral):
    place = lax.axis_index(axis)
    gathered = jax.tree.map(
        lambda a, kind: lax.all_gather(a.astype(kind), axis), x, (jnp.bfloat16, jnp.bfloat16)
    )
    state = jax.tree.map(lambda a, e: jnp.zeros_like(a) + jnp.asarray(e, a.dtype), x, neutral)

    def one(step, state):
        return join(
            state,
            jax.tree.map(
                lambda a, own: lax.dynamic_index_in_dim(a, step, 0, False).astype(own.dtype),
                gathered,
                x,
            ),
        )

    return lax.fori_loop(0, place, one, state)


def passed_along(value, axis, steps):
    count = lax.axis_size(axis)
    first, last = (max(0, -steps), min(count, count - steps))
    return lax.ppermute(value, axis, [(source, source + steps) for source in range(first, last)])


def rms_scaled(values, scale_gain):
    values = values.astype(jnp.float32)
    return (
        values * lax.rsqrt(jnp.mean(values * values, axis=-1, keepdims=True) + epsilon) * scale_gain
    )


def group_terms(group_in):
    group_x, group_b, group_c, group_step, group_rate = group_in
    cumulative = jnp.cumsum(group_rate, axis=0)
    positions = jnp.arange(group_x.shape[0])
    lower_mask = positions[:, None] >= positions[None, :]
    cum_heads = cumulative.T
    differences = cum_heads[:, :, None] - cum_heads[:, None, :]
    decay_mask = jnp.exp(jnp.where(lower_mask[None], differences, -jnp.inf))
    scores = jnp.dot(group_c, group_b.T, preferred_element_type=jnp.float32)
    weights = (scores[None] * decay_mask * group_step.T[:, None, :]).astype(jnp.bfloat16)
    intra_out = jnp.einsum("hts,shp->thp", weights, group_x, preferred_element_type=jnp.float32)
    tail_weight = jnp.exp(cumulative[-1][None, :] - cumulative) * group_step
    weighted_x = (group_x.astype(jnp.float32) * tail_weight[:, :, None]).astype(jnp.bfloat16)
    local_state = jnp.einsum("shp,sn->hpn", weighted_x, group_b, preferred_element_type=jnp.float32)
    return (intra_out, local_state, cumulative)


def link_states(earlier, latter):
    return (earlier[0] + latter[0], jnp.exp(latter[0])[:, None, None] * earlier[1] + latter[1])


def incoming_state(whole_decay, final_state):
    identity = (jnp.zeros_like(whole_decay), jnp.zeros_like(final_state))
    passed = entering_2((whole_decay, final_state), "seq", link_states, identity)
    return passed[1]


def advance(carry_state, group_item):
    group_total, local_state = group_item
    return (jnp.exp(group_total)[:, None, None] * carry_state + local_state, carry_state)


def mixer(
    sequence,
    layer,
    norm_gain,
    in_weight,
    state_weight,
    conv_weight,
    conv_bias,
    step_bias,
    decay_log,
    skip_gain,
    out_gain,
):
    length = sequence.shape[0]
    inner_width = in_weight.shape[2] // 2
    normed = rms_scaled(sequence, norm_gain[layer]).astype(jnp.bfloat16)
    gate_x = jnp.dot(normed, in_weight[layer], preferred_element_type=jnp.float32).astype(
        jnp.bfloat16
    )
    state_proj = jnp.dot(normed, state_weight[layer], preferred_element_type=jnp.float32).astype(
        jnp.bfloat16
    )
    x_part = gate_x[:, inner_width:]
    bc_part = state_proj[:, : 2 * STATE]
    margin = conv_weight.shape[1] - 1
    edge_rows = passed_along((x_part[length - margin :], bc_part[length - margin :]), "seq", 1)
    x_padded = jnp.concatenate([edge_rows[0], x_part], axis=0)
    bc_padded = jnp.concatenate([edge_rows[1], bc_part], axis=0)
    taps = conv_weight[layer]
    conv_x = jnp.zeros((length, inner_width), jnp.float32) + conv_bias[layer][None, :inner_width]
    conv_bc = jnp.zeros((length, 2 * STATE), jnp.float32) + conv_bias[layer][None, inner_width:]
    for offset in range(margin + 1):
        conv_x = conv_x + taps[offset][None, :inner_width] * x_padded[
            offset : offset + length
        ].astype(jnp.float32)
        conv_bc = conv_bc + taps[offset][None, inner_width:] * bc_padded[
            offset : offset + length
        ].astype(jnp.float32)
    x_conv = jax.nn.silu(conv_x).astype(jnp.bfloat16)
    bc_conv = jax.nn.silu(conv_bc).astype(jnp.bfloat16)
    step_size = jax.nn.softplus(
        state_proj[:, 2 * STATE :].astype(jnp.float32) + step_bias[layer][None, :]
    )
    log_rates = -step_size * jnp.exp(decay_log[layer])[None, :]
    group_count = length // GROUP
    group_x = x_conv.reshape(group_count, GROUP, HEADS, HEADDIM)
    group_c = bc_conv[:, STATE:].reshape(group_count, GROUP, STATE)
    inputs = (
        group_x,
        bc_conv[:, :STATE].reshape(group_count, GROUP, STATE),
        group_c,
        step_size.reshape(group_count, GROUP, HEADS),
        log_rates.reshape(group_count, GROUP, HEADS),
    )
    intra_out, local_states, cumulative = lax.map(group_terms, inputs)
    totals = cumulative[:, -1, :]
    final_state, entering = lax.scan(
        advance, jnp.zeros((HEADS, HEADDIM, STATE), jnp.float32), (totals, local_states)
    )
    arriving = incoming_state(jnp.sum(totals, axis=0), final_state)
    before = jnp.cumsum(totals, axis=0) - totals
    start_states = entering + jnp.exp(before)[:, :, None, None] * arriving[None]
    inter_out = jnp.exp(cumulative)[..., None] * jnp.einsum(
        "ctn,chpn->cthp", group_c.astype(jnp.float32), start_states, precision=lax.Precision.HIGHEST
    )
    y_total = (
        intra_out + inter_out + skip_gain[layer][None, None, :, None] * group_x.astype(jnp.float32)
    )
    gated = y_total.reshape(length, inner_width) * jax.nn.silu(
        gate_x[:, :inner_width].astype(jnp.float32)
    )
    return rms_scaled(gated, out_gain[layer]).astype(jnp.bfloat16)


def on_device(
    slide_tiles,
    norm_gain,
    in_weight,
    state_weight,
    conv_weight,
    conv_bias,
    step_bias,
    decay_log,
    skip_gain,
    out_gain,
    out_weight,
):
    row_count, col_count, feature_count = slide_tiles.shape
    params = (
        norm_gain,
        in_weight,
        state_weight,
        conv_weight,
        conv_bias,
        step_bias,
        decay_log,
        skip_gain,
        out_gain,
    )
    flipped = slide_tiles[:, ::-1, :]
    columns = lax.all_to_all(flipped, "seq", split_axis=1, concat_axis=0, tiled=True)
    full_rows, block_cols = (columns.shape[0], columns.shape[1])
    first_order = jnp.transpose(columns[::-1], (1, 0, 2)).reshape(
        full_rows * block_cols, feature_count
    )
    mixed_out = mixer(first_order, 0, *params)
    layer_out = (
        first_order.astype(jnp.float32)
        + jnp.dot(mixed_out, out_weight[0], preferred_element_type=jnp.float32)
    ).astype(jnp.bfloat16)
    row_grid = jnp.transpose(layer_out.reshape(block_cols, full_rows, feature_count), (1, 0, 2))[
        ::-1
    ]
    returned = lax.all_to_all(row_grid, "seq", split_axis=0, concat_axis=1, tiled=True)
    second = returned[:, ::-1, :].reshape(row_count * col_count, feature_count)
    mixed_out = mixer(second, 1, *params)
    result = (
        second.astype(jnp.float32)
        + jnp.dot(mixed_out, out_weight[1], preferred_element_type=jnp.float32)
    ).astype(jnp.bfloat16)
    return result.reshape(row_count, col_count, feature_count)


def solution(mesh):
    placed = (P(("dp", "seq"), None, None), P(), P(), P(), P(), P(), P(), P(), P(), P(), P())
    return jax.shard_map(
        on_device,
        mesh=mesh,
        in_specs=placed,
        out_specs=P(("dp", "seq"), None, None),
        check_vma=False,
    )
```

profile of v0, /device:TPU:0, one launch (start us, length us, event | category | flops | bytes accessed | tf_op | source)
XLA Modules:
  0.0 138.6 jit_solution(18102543792137817311)
XLA Ops:
  0.1 1.5 %copy.98 = bf16[2,256,384]{2,0,1:T(2,128)(2,1)S(1)} copy(bf16[2,256,384]{2,1,0:T(8,128)(2,1)} %param.23) | data formatting | bytes 786432 | tf_op args[0]
  2.5 5.2 %all-to-all-start = ((bf16[2,256,384]{2,0,1:T(2,128)(2,1)}), bf16[2,256,384]{2,0,1:T(2,128)(2,1)S(1)}, u32[]{:S(2)}, u32[]{:S(2)}) async-start(bf16[2,256,384]{2,0,1:T(2,128)(2,1)} %rev.12), calls=%async_computation | async-start | bytes 786432 | tf_op jit(solution)/shard_map/all_to_all | solution.py:178
  14.3 1.7 %all-to-all-done = bf16[2,256,384]{2,0,1:T(2,128)(2,1)S(1)} async-done(((bf16[2,256,384]{2,0,1:T(2,128)(2,1)}), bf16[2,256,384]{2,0,1:T(2,128)(2,1)S(1)}, u32[]{:S(2)}, u32[]{:S(2)}) %all-to-all-start) | async-done | bytes 393248 | tf_op jit(solution)/shard_map/all_to_all | solution.py:178
  17.5 2.3 %convolution_convert_fusion.1 = bf16[512,1536]{1,0:T(8,128)(2,1)S(1)} fusion(bf16[512,384]{1,0:T(8,128)(2,1)S(1)} %bitcast.348, bf16[2,384,1536]{2,1,0:T(8,128)(2,1)} %param.25), kind=kOutput, calls=%fused_computation.95 | convolution fusion | flops 604766208 | bytes 3145728 | tf_op jit(solution)/shard_map/dot_general | solution.py:94
  21.1 1.3 collective-permute-start.1
  22.4 3.2 %collective-permute-start = (bf16[3,768]{1,0:T(4,128)(2,1)S(1)}, bf16[3,768]{1,0:T(4,128)(2,1)S(1)}, u32[]{:S(2)}, u32[]{:S(2)}) collective-permute-start(bf16[3,768]{1,0:T(4,128)(2,1)S(1)} %slice.368), channel_id=1, source_target_pairs={{0,1},{1,2},{2,3},{3,4},{4,5},{5,6},{6,7},{8,9},{9,10},{10,11},{11... | collective-permute-start | bytes 13832 | tf_op jit(solution)/shard_map/ppermute | solution.py:36
  29.1 8.0 %while.78 = (s32[]{:T(128)}, f32[2,256,12,64]{1,3,2,0:T(8,128)S(1)}, f32[2,12,64,16]{2,3,1,0:T(8,128)S(1)}, f32[2,256,12]{1,2,0:T(8,128)}, bf16[2,256,12,64]{1,3...) while((s32[]{:T(128)}, ...), condition=%wide.region_4.5_spmd, body=%wide.region_1.4_spmd.sunk | while | flops 114038824 | bytes 2966549 | solution.py:132
  39.2 10.9 %all-gather.1 = bf16[96,64,16]{1,2,0:T(8,128)(2,1)S(1)} all-gather(bf16[12,64,16]{1,2,0:T(8,128)(2,1)S(1)} %convert_element_type.257), channel_id=3, replica_groups=mesh['dp'=4,'seq'=8] {'seq'}, dimensions={0}, use_global_device_ids=true | all-gather | bytes 221184 | tf_op jit(solution)/shard_map/all_gather | solution.py:16
  50.3 13.2 %all-reduce = bf16[96]{0:T(256)(128)(2,1)S(1)} all-reduce(bf16[96]{0:T(256)(128)(2,1)S(1)} %dynamic-update-slice), channel_id=2, replica_groups=mesh['dp'=4,'seq'=8] {'seq'}, use_global_device_ids=true, to_apply=%add | all-reduce | flops 96 | bytes 384
  63.9 1.3 multiply_add_fusion.1
  65.2 1.2 copy.109
  67.1 1.9 %multiply_reduce_fusion.1 = f32[512]{0:T(512)S(1)} fusion(f32[512,768]{1,0:T(8,128)S(1)} %copy.110, bf16[512,1536]{1,0:T(8,128)(2,1)} %copy-done.4), kind=kLoop, calls=%fused_computation.113 | loop fusion | flops 3145216 | bytes 2361344 | tf_op jit(solution)/shard_map/reduce_sum | solution.py:42
  68.9 1.9 %fusion.68 = bf16[512,384]{1,0:T(8,128)(2,1)S(1)} fusion(f32[512,384]{1,0:T(8,128)S(1)} %bitcast.351, f32[768]{0:T(1024)S(1)} %copy-done.25, f32[512]{0:T(512)S(1)} %add_rsqrt_fusion.3, bf16[2,768,384]{2,1,0:T(8,128)(2,1)} %param.33, f32[512,768]{1,0:T(8,128)S(1)} %copy.110, bf16[512,1536]{1,0:T(8,128)(2,1)S(1)} %copy-done.5), kind=kOutput, calls=%fused_computation.118 | convolution fusion | flops 305922048 | bytes 4134912 | tf_op jit(solution)/shard_map/dot_general | solution.py:186
  71.7 3.6 %all-to-all-start.1 = ((bf16[16,32,384]{2,1,0:T(8,128)(2,1)}), bf16[16,32,384]{2,1,0:T(8,128)(2,1)S(1)}, u32[]{:S(2)}, u32[]{:S(2)}) async-start(bf16[16,32,384]{2,1,0:T(8,128)(2,1)} %rev.14), calls=%async_computation.1 | async-start | bytes 786432 | tf_op jit(solution)/shard_map/all_to_all | solution.py:191
  75.3 8.2 %all-to-all-done.1 = bf16[16,32,384]{2,1,0:T(8,128)(2,1)S(1)} async-done(((bf16[16,32,384]{2,1,0:T(8,128)(2,1)}), bf16[16,32,384]{2,1,0:T(8,128)(2,1)S(1)}, u32[]{:S(2)}, u32[]{:S(2)}) %all-to-all-start.1) | async-done | bytes 393248 | tf_op jit(solution)/shard_map/all_to_all | solution.py:191
  84.8 2.3 %convolution_convert_fusion = bf16[512,1536]{1,0:T(8,128)(2,1)S(1)} fusion(bf16[512,384]{1,0:T(8,128)(2,1)S(1)} %bitcast.346, bf16[2,384,1536]{2,1,0:T(8,128)(2,1)} %param.25), kind=kOutput, calls=%fused_computation.94 | convolution fusion | flops 604766208 | bytes 3145728 | tf_op jit(solution)/shard_map/dot_general | solution.py:94
  88.2 1.3 collective-permute-start.3
  89.5 3.2 %collective-permute-start.2 = (bf16[3,768]{1,0:T(4,128)(2,1)S(1)}, bf16[3,768]{1,0:T(4,128)(2,1)S(1)}, u32[]{:S(2)}, u32[]{:S(2)}) collective-permute-start(bf16[3,768]{1,0:T(4,128)(2,1)S(1)} %slice.384), channel_id=1, source_target_pairs={{0,1},{1,2},{2,3},{3,4},{4,5},{5,6},{6,7},{8,9},{9,10},{10,11},{11... | collective-permute-start | bytes 13832 | tf_op jit(solution)/shard_map/ppermute | solution.py:36
  96.2 7.9 %while.80 = (s32[]{:T(128)}, f32[2,256,12,64]{1,3,2,0:T(8,128)S(1)}, f32[2,12,64,16]{2,3,1,0:T(8,128)S(1)}, f32[2,256,12]{1,2,0:T(8,128)}, bf16[2,256,12,64]{1,3...) while((s32[]{:T(128)}, ...), condition=%wide.region_16.17_spmd, body=%wide.region_13.16_spmd.sunk | while | flops 114038824 | bytes 2966549 | solution.py:132
  106.3 10.8 %all-gather.3 = bf16[96,64,16]{1,2,0:T(8,128)(2,1)S(1)} all-gather(bf16[12,64,16]{1,2,0:T(8,128)(2,1)S(1)} %convert_element_type.282), channel_id=5, replica_groups=mesh['dp'=4,'seq'=8] {'seq'}, dimensions={0}, use_global_device_ids=true | all-gather | bytes 221184 | tf_op jit(solution)/shard_map/all_gather | solution.py:16
  117.3 13.2 %all-reduce.1 = bf16[96]{0:T(256)(128)(2,1)S(1)} all-reduce(bf16[96]{0:T(256)(128)(2,1)S(1)} %dynamic-update-slice.1), channel_id=4, replica_groups=mesh['dp'=4,'seq'=8] {'seq'}, use_global_device_ids=true, to_apply=%add.1 | all-reduce | flops 96 | bytes 384
  130.9 1.3 multiply_add_fusion
  134.1 1.8 %multiply_reduce_fusion = f32[512]{0:T(512)S(1)} fusion(f32[512,768]{1,0:T(8,128)S(1)} %copy.123, bf16[512,1536]{1,0:T(8,128)(2,1)} %copy-done.2), kind=kLoop, calls=%fused_computation.109 | loop fusion | flops 3145216 | bytes 2361344 | tf_op jit(solution)/shard_map/reduce_sum | solution.py:42
  136.0 2.6 %fusion.69 = bf16[512,384]{1,0:T(8,128)(2,1)} fusion(f32[768]{0:T(1024)S(1)} %copy-done.24, f32[512]{0:T(512)S(1)} %add_rsqrt_fusion.1, bf16[2,768,384]{2,1,0:T(8,128)(2,1)} %param.33, f32[512,768]{1,0:T(8,128)S(1)} %copy.123, bf16[512,1536]{1,0:T(8,128)(2,1)S(1)} %copy-done.3, bf16[512,384]{1,0:T(8,128)(2,1)S(1)} %bitcast.336), kind=kOutput, calls=%fused_computation.119 | convolution fusion | flops 306118656 | bytes 3741696 | tf_op jit(solution)/shard_map/dot_general | solution.py:196
  (281 shorter events, 43.3 us)
Async XLA Ops:
  0.0 11.8 %copy-start.39 = (u32[32]{0:T(128)S(1)}, u32[32]{0:T(128)}, u32[]{:S(2)}) copy-start(u32[32]{0:T(128)} %constant.128) | copy-start | bytes 388
  0.0 7.7 %copy-start.22 = (f32[2,800]{1,0:T(2,128)S(1)}, f32[2,800]{1,0:T(2,128)}, u32[]{:S(2)}) copy-start(f32[2,800]{1,0:T(2,128)} %param.28) | copy-start | bytes 19204
  0.0 8.9 %copy-start.26 = (f32[2,384]{1,0:T(2,128)S(1)}, f32[2,384]{1,0:T(2,128)}, u32[]{:S(2)}) copy-start(f32[2,384]{1,0:T(2,128)} %param.24) | copy-start | bytes 9220
  0.0 9.5 %copy-start.15 = (f32[2,4,800]{2,1,0:T(4,128)S(1)}, f32[2,4,800]{2,1,0:T(4,128)}, u32[]{:S(2)}) copy-start(f32[2,4,800]{2,1,0:T(4,128)} %param.27) | copy-start | bytes 76804
  0.0 10.1 %copy-start.36 = (f32[2,12]{1,0:T(2,128)S(1)}, f32[2,12]{1,0:T(2,128)}, u32[]{:S(2)}) copy-start(f32[2,12]{1,0:T(2,128)} %param.31) | copy-start | bytes 292
  0.0 10.6 %copy-start.23 = (f32[2,768]{1,0:T(2,128)S(1)}, f32[2,768]{1,0:T(2,128)}, u32[]{:S(2)}) copy-start(f32[2,768]{1,0:T(2,128)} %param.32) | copy-start | bytes 18436
  0.0 11.2 %copy-start.38 = (f32[2,12]{1,0:T(2,128)S(1)}, f32[2,12]{1,0:T(2,128)}, u32[]{:S(2)}) copy-start(f32[2,12]{1,0:T(2,128)} %param.29) | copy-start | bytes 292
  0.0 11.2 %copy-start.37 = (f32[2,12]{1,0:T(2,128)S(1)}, f32[2,12]{1,0:T(2,128)}, u32[]{:S(2)}) copy-start(f32[2,12]{1,0:T(2,128)} %param.30) | copy-start | bytes 292
  0.0 13.6 %copy-start.11 = (bf16[2,384,44]{1,0,2:T(2,128)(2,1)S(1)}, bf16[2,384,44]{1,0,2:T(2,128)(2,1)}, u32[]{:S(2)}) copy-start(bf16[2,384,44]{1,0,2:T(2,128)(2,1)} %param.26) | copy-start | bytes 202756
  2.5 13.5 %all-to-all-start = ((bf16[2,256,384]{2,0,1:T(2,128)(2,1)}), bf16[2,256,384]{2,0,1:T(2,128)(2,1)S(1)}, u32[]{:S(2)}, u32[]{:S(2)}) async-start(bf16[2,256,384]{2,0,1:T(2,128)(2,1)} %rev.12), calls=%async_computation | async-start | bytes 786432 | tf_op jit(solution)/shard_map/all_to_all | solution.py:178
  21.1 4.6 %collective-permute-start.1 = (bf16[3,32]{0,1:T(8,128)(2,1)S(1)}, bf16[3,32]{0,1:T(8,128)(2,1)S(1)}, u32[]{:S(2)}, u32[]{:S(2)}) collective-permute-start(bf16[3,32]{0,1:T(8,128)(2,1)S(1)} %slice.374), channel_id=1, source_target_pairs={{0,1},{1,2},{2,3},{3,4},{4,5},{5,6},{6,7},{8,9},{9,10},{10,11},{11... | collective-permute-start | bytes 584 | tf_op jit(solution)/shard_map/ppermute | solution.py:36
  22.4 4.2 %collective-permute-start = (bf16[3,768]{1,0:T(4,128)(2,1)S(1)}, bf16[3,768]{1,0:T(4,128)(2,1)S(1)}, u32[]{:S(2)}, u32[]{:S(2)}) collective-permute-start(bf16[3,768]{1,0:T(4,128)(2,1)S(1)} %slice.368), channel_id=1, source_target_pairs={{0,1},{1,2},{2,3},{3,4},{4,5},{5,6},{6,7},{8,9},{9,10},{10,11},{11... | collective-permute-start | bytes 13832 | tf_op jit(solution)/shard_map/ppermute | solution.py:36
  39.2 24.7 %copy-start.14 = (bf16[2,256,16]{1,0,2:T(2,128)(2,1)S(1)}, bf16[2,256,16]{1,0,2:T(2,128)(2,1)}, u32[]{:S(2)}) copy-start(bf16[2,256,16]{1,0,2:T(2,128)(2,1)} %reshape.377) | copy-start | bytes 49156
  39.2 24.7 %copy-start.33 = (f32[12]{0:T(128)S(1)}, f32[12]{0:T(128)}, u32[]{:S(2)}) copy-start(f32[12]{0:T(128)} %get-tuple-element.486) | copy-start | bytes 148
  71.7 12.6 %copy-start.21 = (f32[384]{0:T(512)S(1)}, f32[384]{0:T(512)}, u32[]{:S(2)}) copy-start(f32[384]{0:T(512)} %get-tuple-element.383) | copy-start | bytes 4612
  71.7 11.8 %all-to-all-start.1 = ((bf16[16,32,384]{2,1,0:T(8,128)(2,1)}), bf16[16,32,384]{2,1,0:T(8,128)(2,1)S(1)}, u32[]{:S(2)}, u32[]{:S(2)}) async-start(bf16[16,32,384]{2,1,0:T(8,128)(2,1)} %rev.14), calls=%async_computation.1 | async-start | bytes 786432 | tf_op jit(solution)/shard_map/all_to_all | solution.py:191
  75.3 9.2 %copy-start.12 = (bf16[1,384,44]{1,0,2:T(2,128)(2,1)S(1)}, bf16[1,384,44]{1,0,2:T(2,128)(2,1)}, u32[]{:S(2)}) copy-start(bf16[1,384,44]{1,0,2:T(2,128)(2,1)} %get-tuple-element.465) | copy-start | bytes 101380
  87.1 6.6 %copy-start.16 = (f32[768]{0:T(1024)S(1)}, f32[768]{0:T(1024)}, u32[]{:S(2)}) copy-start(f32[768]{0:T(1024)} %get-tuple-element.371) | copy-start | bytes 9220
  87.1 6.6 %copy-start.17 = (f32[768]{0:T(1024)S(1)}, f32[768]{0:T(1024)}, u32[]{:S(2)}) copy-start(f32[768]{0:T(1024)} %get-tuple-element.372) | copy-start | bytes 9220
  87.1 6.6 %copy-start.18 = (f32[768]{0:T(1024)S(1)}, f32[768]{0:T(1024)}, u32[]{:S(2)}) copy-start(f32[768]{0:T(1024)} %get-tuple-element.373) | copy-start | bytes 9220
  88.2 4.7 %collective-permute-start.3 = (bf16[3,32]{0,1:T(8,128)(2,1)S(1)}, bf16[3,32]{0,1:T(8,128)(2,1)S(1)}, u32[]{:S(2)}, u32[]{:S(2)}) collective-permute-start(bf16[3,32]{0,1:T(8,128)(2,1)S(1)} %slice.390), channel_id=1, source_target_pairs={{0,1},{1,2},{2,3},{3,4},{4,5},{5,6},{6,7},{8,9},{9,10},{10,11},{11... | collective-permute-start | bytes 584 | tf_op jit(solution)/shard_map/ppermute | solution.py:36
  89.5 4.2 %collective-permute-start.2 = (bf16[3,768]{1,0:T(4,128)(2,1)S(1)}, bf16[3,768]{1,0:T(4,128)(2,1)S(1)}, u32[]{:S(2)}, u32[]{:S(2)}) collective-permute-start(bf16[3,768]{1,0:T(4,128)(2,1)S(1)} %slice.384), channel_id=1, source_target_pairs={{0,1},{1,2},{2,3},{3,4},{4,5},{5,6},{6,7},{8,9},{9,10},{10,11},{11... | collective-permute-start | bytes 13832 | tf_op jit(solution)/shard_map/ppermute | solution.py:36
  106.3 24.7 %copy-start.13 = (bf16[2,256,16]{1,0,2:T(2,128)(2,1)S(1)}, bf16[2,256,16]{1,0,2:T(2,128)(2,1)}, u32[]{:S(2)}) copy-start(bf16[2,256,16]{1,0,2:T(2,128)(2,1)} %reshape.384) | copy-start | bytes 49156
  106.3 24.7 %copy-start.31 = (f32[12]{0:T(128)S(1)}, f32[12]{0:T(128)}, u32[]{:S(2)}) copy-start(f32[12]{0:T(128)} %get-tuple-element.485) | copy-start | bytes 148
  (26 other events, 81.3 us)
where the time goes:
time: 140 us; the launch traced here: 139 us
  blocking collectives  48.3 us (34%)
  local copies, waits for them, and re-layouts  28.6 us (20%)
  matrix products  17.9 us (13%)
  starting transfers between devices  17.7 us (13%)
  other arithmetic  13.7 us (10%)
  waiting for transfers between devices  9.95 us (7%)
  between operations  1.55 us (1%)
    unnamed x2, blocking collectives  26.5 us
    all_gather x2, blocking collectives, entering_2(): lax.all_gather(a.astype(kind), axis)  21.8 us
    ppermute x4, starting transfers between devices, passed_along(): lax.ppermute(value, axis, [(source, source + steps) for source in range(f...  8.94 us
    all_to_all x1, waiting for transfers between devices, on_device(): lax.all_to_all(row_grid, 'seq', split_axis=0, concat_axis=1, tiled=True)  8.22 us
    all_to_all x1, starting transfers between devices, on_device(): lax.all_to_all(flipped, 'seq', split_axis=1, concat_axis=0, tiled=True)  5.2 us
    dot_general x2, matrix products, mixer(): jnp.dot(normed, in_weight[layer], preferred_element_type=jnp.float32)  4.51 us
    unnamed x80, local copies, waits for them, and re-layouts  4.07 us
    reduce_sum x4, other arithmetic, rms_scaled(): jnp.mean(values * values, axis=-1, keepdims=True) + epsilon  3.99 us
  transfers between devices with their start and end apart: 6, of which 2 were waited for; matrix products, arithmetic and copies ran while one was open for 6% of the time, Pallas kernels for 0%

commit v1 on v0

--- a/solution.py
+++ b/solution.py
@@ -8,6 +8,15 @@
 STATE = 16
 GROUP = 256
 epsilon = 1e-05
+views_save = lambda mine: jnp.concatenate(
+    lax.all_to_all(
+        jnp.stack(jnp.split(mine, lax.psum(1, "seq"), axis=0), axis=0),
+        split_axis=0,
+        axis_name="seq",
+        concat_axis=0,
+    ),
+    axis=1,
+)
 
 
 def entering_2(x, axis, join, neutral):
@@ -188,7 +197,7 @@
     row_grid = jnp.transpose(layer_out.reshape(block_cols, full_rows, feature_count), (1, 0, 2))[
         ::-1
     ]
-    returned = lax.all_to_all(row_grid, "seq", split_axis=0, concat_axis=1, tiled=True)
+    returned = views_save(row_grid)
     second = returned[:, ::-1, :].reshape(row_count * col_count, feature_count)
     mixed_out = mixer(second, 1, *params)
     result = (

time: 140 us -> 148 us (1.057)
  local copies, waits for them, and re-layouts: 28.6 us -> 37.7 us
    unnamed x80 -> x87, local copies, waits for them, and re-layouts: 4.07 us -> 8.64 us
    dynamic_slice x12, local copies, waits for them, and re-layouts: 0.13 us -> 3.07 us  [mixer(): intra_out, local_states, cumulative = lax.map(group_terms, inputs)]
    split x0 -> x9, local copies, waits for them, and re-layouts: none -> 2.9 us  [jnp.split(mine, lax.psum(1, 'seq'), axis=0)]
    while x24 -> x8, local copies, waits for them, and re-layouts: 2.31 us -> 0.05 us
where the time goes in v1:
time: 148 us; the launch traced here: 146 us
  blocking collectives  47.3 us (32%)
  local copies, waits for them, and re-layouts  37.7 us (25%)
  matrix products  17.9 us (12%)
  starting transfers between devices  17.6 us (12%)
  other arithmetic  13.7 us (9%)
  waiting for transfers between devices  10 us (7%)
  between operations  1.55 us (1%)
    unnamed x2, blocking collectives  26.7 us
    all_gather x2, blocking collectives, entering_2(): lax.all_gather(a.astype(kind), axis)  20.6 us
    ppermute x4, starting transfers between devices, passed_along(): lax.ppermute(value, axis, [(source, source + steps) for source in range(f...  8.95 us
    unnamed x87, local copies, waits for them, and re-layouts  8.64 us
    all_to_all x1, waiting for transfers between devices, lax.all_to_all(jnp.stack(jnp.split(mine, lax.psum(1, 'seq'), axis=0), axi...  8.22 us
    all_to_all x1, starting transfers between devices, on_device(): lax.all_to_all(flipped, 'seq', split_axis=1, concat_axis=0, tiled=True)  5.2 us
    dot_general x2, matrix products, mixer(): jnp.dot(normed, in_weight[layer], preferred_element_type=jnp.float32)  4.49 us
    reduce_sum x4, other arithmetic, rms_scaled(): jnp.mean(values * values, axis=-1, keepdims=True) + epsilon  3.99 us
  transfers between devices with their start and end apart: 6, of which 2 were waited for; matrix products, arithmetic and copies ran while one was open for 6% of the time, Pallas kernels for 0%

profile of v1, /device:TPU:0, one launch (start us, length us, event | category | flops | bytes accessed | tf_op | source)
XLA Modules:
  0.0 146.5 jit_solution(9471441603950000450)
XLA Ops:
  0.1 1.5 %copy.98 = bf16[2,256,384]{2,0,1:T(2,128)(2,1)S(1)} copy(bf16[2,256,384]{2,1,0:T(8,128)(2,1)} %param.23) | data formatting | bytes 786432 | tf_op args[0]
  2.5 5.2 %all-to-all-start = ((bf16[2,256,384]{2,0,1:T(2,128)(2,1)}), bf16[2,256,384]{2,0,1:T(2,128)(2,1)S(1)}, u32[]{:S(2)}, u32[]{:S(2)}) async-start(bf16[2,256,384]{2,0,1:T(2,128)(2,1)} %rev.10), calls=%async_computation | async-start | bytes 786432 | tf_op jit(solution)/shard_map/all_to_all | solution.py:187
  14.3 1.8 %all-to-all-done = bf16[2,256,384]{2,0,1:T(2,128)(2,1)S(1)} async-done(((bf16[2,256,384]{2,0,1:T(2,128)(2,1)}), bf16[2,256,384]{2,0,1:T(2,128)(2,1)S(1)}, u32[]{:S(2)}, u32[]{:S(2)}) %all-to-all-start) | async-done | bytes 393248 | tf_op jit(solution)/shard_map/all_to_all | solution.py:187
  17.5 2.2 %convolution_convert_fusion.1 = bf16[512,1536]{1,0:T(8,128)(2,1)S(1)} fusion(bf16[512,384]{1,0:T(8,128)(2,1)S(1)} %bitcast.360, bf16[2,384,1536]{2,1,0:T(8,128)(2,1)} %param.25), kind=kOutput, calls=%fused_computation.95 | convolution fusion | flops 604766208 | bytes 3145728 | tf_op jit(solution)/shard_map/dot_general | solution.py:103
  21.1 1.3 collective-permute-start.1
  22.4 3.2 %collective-permute-start = (bf16[3,768]{1,0:T(4,128)(2,1)S(1)}, bf16[3,768]{1,0:T(4,128)(2,1)S(1)}, u32[]{:S(2)}, u32[]{:S(2)}) collective-permute-start(bf16[3,768]{1,0:T(4,128)(2,1)S(1)} %slice.376), channel_id=1, source_target_pairs={{0,1},{1,2},{2,3},{3,4},{4,5},{5,6},{6,7},{8,9},{9,10},{10,11},{11... | collective-permute-start | bytes 13832 | tf_op jit(solution)/shard_map/ppermute | solution.py:45
  29.7 8.3 %while.78 = (s32[]{:T(128)}, f32[2,256,12,64]{1,3,2,0:T(8,128)S(1)}, f32[2,12,64,16]{2,3,1,0:T(8,128)S(1)}, f32[2,256,12]{1,2,0:T(8,128)}, bf16[2,256,12,64]{1,3...) while((s32[]{:T(128)}, ...), condition=%wide.region_4.5_spmd, body=%wide.region_1.4_spmd.sunk | while | flops 114038824 | bytes 2769885 | solution.py:141
  40.1 10.3 %all-gather.1 = bf16[96,64,16]{1,2,0:T(8,128)(2,1)S(1)} all-gather(bf16[12,64,16]{1,2,0:T(8,128)(2,1)S(1)} %convert_element_type.257), channel_id=3, replica_groups=mesh['dp'=4,'seq'=8] {'seq'}, dimensions={0}, use_global_device_ids=true | all-gather | bytes 221184 | tf_op jit(solution)/shard_map/all_gather | solution.py:25
  50.6 13.2 %all-reduce = bf16[96]{0:T(256)(128)(2,1)S(1)} all-reduce(bf16[96]{0:T(256)(128)(2,1)S(1)} %dynamic-update-slice), channel_id=2, replica_groups=mesh['dp'=4,'seq'=8] {'seq'}, use_global_device_ids=true, to_apply=%add | all-reduce | flops 96 | bytes 384
  64.2 1.3 multiply_add_fusion.1
  65.5 1.2 copy.109
  67.4 1.9 %multiply_reduce_fusion.1 = f32[512]{0:T(512)S(1)} fusion(f32[512,768]{1,0:T(8,128)S(1)} %copy.110, bf16[512,1536]{1,0:T(8,128)(2,1)} %copy-done.4), kind=kLoop, calls=%fused_computation.113 | loop fusion | flops 3145216 | bytes 2361344 | tf_op jit(solution)/shard_map/reduce_sum | solution.py:51
  69.3 1.9 %fusion.68 = bf16[512,384]{1,0:T(8,128)(2,1)S(1)} fusion(f32[512,384]{1,0:T(8,128)S(1)} %bitcast.363, f32[768]{0:T(1024)S(1)} %copy-done.21, f32[512]{0:T(512)S(1)} %add_rsqrt_fusion.3, bf16[2,768,384]{2,1,0:T(8,128)(2,1)} %param.33, f32[512,768]{1,0:T(8,128)S(1)} %copy.110, bf16[512,1536]{1,0:T(8,128)(2,1)S(1)} %copy-done.5), kind=kOutput, calls=%fused_computation.118 | convolution fusion | flops 305922048 | bytes 4134912 | tf_op jit(solution)/shard_map/dot_general | solution.py:195
  79.3 3.5 %all-to-all-start.1 = ((bf16[8,2,32,384]{3,1,2,0:T(2,128)(2,1)}), bf16[8,2,32,384]{3,1,2,0:T(2,128)(2,1)S(1)}, u32[]{:S(2)}, u32[]{:S(2)}) async-start(bf16[8,2,32,384]{3,1,2,0:T(2,128)(2,1)} %bitcast_dynamic-update-slice_fusion.4), calls=%async_computation.1 | async-start | bytes 786432 | tf_op jit(solution)/shard_map/all_to_all | solution.py:12
  82.8 8.2 %all-to-all-done.1 = bf16[8,2,32,384]{3,1,2,0:T(2,128)(2,1)S(1)} async-done(((bf16[8,2,32,384]{3,1,2,0:T(2,128)(2,1)}), bf16[8,2,32,384]{3,1,2,0:T(2,128)(2,1)S(1)}, u32[]{:S(2)}, u32[]{:S(2)}) %all-to-all-start.1) | async-done | bytes 393248 | tf_op jit(solution)/shard_map/all_to_all | solution.py:12
  92.3 2.2 %convolution_convert_fusion = bf16[512,1536]{1,0:T(8,128)(2,1)S(1)} fusion(bf16[512,384]{1,0:T(8,128)(2,1)S(1)} %bitcast.358, bf16[2,384,1536]{2,1,0:T(8,128)(2,1)} %param.25), kind=kOutput, calls=%fused_computation.94 | convolution fusion | flops 604766208 | bytes 3145728 | tf_op jit(solution)/shard_map/dot_general | solution.py:103
  95.7 1.3 collective-permute-start.3
  97.0 3.2 %collective-permute-start.2 = (bf16[3,768]{1,0:T(4,128)(2,1)S(1)}, bf16[3,768]{1,0:T(4,128)(2,1)S(1)}, u32[]{:S(2)}, u32[]{:S(2)}) collective-permute-start(bf16[3,768]{1,0:T(4,128)(2,1)S(1)} %slice.392), channel_id=1, source_target_pairs={{0,1},{1,2},{2,3},{3,4},{4,5},{5,6},{6,7},{8,9},{9,10},{10,11},{11... | collective-permute-start | bytes 13832 | tf_op jit(solution)/shard_map/ppermute | solution.py:45
  104.3 8.3 %while.80 = (s32[]{:T(128)}, f32[2,256,12,64]{1,3,2,0:T(8,128)S(1)}, f32[2,12,64,16]{2,3,1,0:T(8,128)S(1)}, f32[2,256,12]{1,2,0:T(8,128)}, bf16[2,256,12,64]{1,3...) while((s32[]{:T(128)}, ...), condition=%wide.region_16.17_spmd, body=%wide.region_13.16_spmd.sunk | while | flops 114038824 | bytes 2769885 | solution.py:141
  114.7 10.3 %all-gather.3 = bf16[96,64,16]{1,2,0:T(8,128)(2,1)S(1)} all-gather(bf16[12,64,16]{1,2,0:T(8,128)(2,1)S(1)} %convert_element_type.282), channel_id=5, replica_groups=mesh['dp'=4,'seq'=8] {'seq'}, dimensions={0}, use_global_device_ids=true | all-gather | bytes 221184 | tf_op jit(solution)/shard_map/all_gather | solution.py:25
  125.2 13.5 %all-reduce.1 = bf16[96]{0:T(256)(128)(2,1)S(1)} all-reduce(bf16[96]{0:T(256)(128)(2,1)S(1)} %dynamic-update-slice.1), channel_id=4, replica_groups=mesh['dp'=4,'seq'=8] {'seq'}, use_global_device_ids=true, to_apply=%add.1 | all-reduce | flops 96 | bytes 384
  138.8 1.3 multiply_add_fusion
  142.0 1.8 %multiply_reduce_fusion = f32[512]{0:T(512)S(1)} fusion(f32[512,768]{1,0:T(8,128)S(1)} %copy.122, bf16[512,1536]{1,0:T(8,128)(2,1)} %copy-done.2), kind=kLoop, calls=%fused_computation.109 | loop fusion | flops 3145216 | bytes 2361344 | tf_op jit(solution)/shard_map/reduce_sum | solution.py:51
  143.9 2.6 %fusion.69 = bf16[512,384]{1,0:T(8,128)(2,1)} fusion(f32[768]{0:T(1024)S(1)} %copy-done.20, f32[512]{0:T(512)S(1)} %add_rsqrt_fusion.1, bf16[2,768,384]{2,1,0:T(8,128)(2,1)} %param.33, f32[512,768]{1,0:T(8,128)S(1)} %copy.122, bf16[512,1536]{1,0:T(8,128)(2,1)S(1)} %copy-done.3, bf16[512,384]{1,0:T(8,128)(2,1)S(1)} %bitcast.350), kind=kOutput, calls=%fused_computation.119 | convolution fusion | flops 306118656 | bytes 3741696 | tf_op jit(solution)/shard_map/dot_general | solution.py:205
  (280 shorter events, 52.2 us)
Async XLA Ops:
  0.0 11.8 %copy-start.35 = (u32[32]{0:T(128)S(1)}, u32[32]{0:T(128)}, u32[]{:S(2)}) copy-start(u32[32]{0:T(128)} %constant.128) | copy-start | bytes 388
  0.0 7.7 %copy-start.18 = (f32[2,800]{1,0:T(2,128)S(1)}, f32[2,800]{1,0:T(2,128)}, u32[]{:S(2)}) copy-start(f32[2,800]{1,0:T(2,128)} %param.28) | copy-start | bytes 19204
  0.0 8.9 %copy-start.22 = (f32[2,384]{1,0:T(2,128)S(1)}, f32[2,384]{1,0:T(2,128)}, u32[]{:S(2)}) copy-start(f32[2,384]{1,0:T(2,128)} %param.24) | copy-start | bytes 9220
  0.0 9.5 %copy-start.11 = (f32[2,4,800]{2,1,0:T(4,128)S(1)}, f32[2,4,800]{2,1,0:T(4,128)}, u32[]{:S(2)}) copy-start(f32[2,4,800]{2,1,0:T(4,128)} %param.27) | copy-start | bytes 76804
  0.0 10.1 %copy-start.32 = (f32[2,12]{1,0:T(2,128)S(1)}, f32[2,12]{1,0:T(2,128)}, u32[]{:S(2)}) copy-start(f32[2,12]{1,0:T(2,128)} %param.31) | copy-start | bytes 292
  0.0 10.6 %copy-start.19 = (f32[2,768]{1,0:T(2,128)S(1)}, f32[2,768]{1,0:T(2,128)}, u32[]{:S(2)}) copy-start(f32[2,768]{1,0:T(2,128)} %param.32) | copy-start | bytes 18436
  0.0 11.2 %copy-start.34 = (f32[2,12]{1,0:T(2,128)S(1)}, f32[2,12]{1,0:T(2,128)}, u32[]{:S(2)}) copy-start(f32[2,12]{1,0:T(2,128)} %param.29) | copy-start | bytes 292
  0.0 11.2 %copy-start.33 = (f32[2,12]{1,0:T(2,128)S(1)}, f32[2,12]{1,0:T(2,128)}, u32[]{:S(2)}) copy-start(f32[2,12]{1,0:T(2,128)} %param.30) | copy-start | bytes 292
  0.0 13.5 %copy-start.7 = (bf16[2,384,44]{1,0,2:T(2,128)(2,1)S(1)}, bf16[2,384,44]{1,0,2:T(2,128)(2,1)}, u32[]{:S(2)}) copy-start(bf16[2,384,44]{1,0,2:T(2,128)(2,1)} %param.26) | copy-start | bytes 202756
  2.5 13.5 %all-to-all-start = ((bf16[2,256,384]{2,0,1:T(2,128)(2,1)}), bf16[2,256,384]{2,0,1:T(2,128)(2,1)S(1)}, u32[]{:S(2)}, u32[]{:S(2)}) async-start(bf16[2,256,384]{2,0,1:T(2,128)(2,1)} %rev.10), calls=%async_computation | async-start | bytes 786432 | tf_op jit(solution)/shard_map/all_to_all | solution.py:187
  21.1 5.3 %collective-permute-start.1 = (bf16[3,32]{0,1:T(8,128)(2,1)S(1)}, bf16[3,32]{0,1:T(8,128)(2,1)S(1)}, u32[]{:S(2)}, u32[]{:S(2)}) collective-permute-start(bf16[3,32]{0,1:T(8,128)(2,1)S(1)} %slice.382), channel_id=1, source_target_pairs={{0,1},{1,2},{2,3},{3,4},{4,5},{5,6},{6,7},{8,9},{9,10},{10,11},{11... | collective-permute-start | bytes 584 | tf_op jit(solution)/shard_map/ppermute | solution.py:45
  22.4 4.8 %collective-permute-start = (bf16[3,768]{1,0:T(4,128)(2,1)S(1)}, bf16[3,768]{1,0:T(4,128)(2,1)S(1)}, u32[]{:S(2)}, u32[]{:S(2)}) collective-permute-start(bf16[3,768]{1,0:T(4,128)(2,1)S(1)} %slice.376), channel_id=1, source_target_pairs={{0,1},{1,2},{2,3},{3,4},{4,5},{5,6},{6,7},{8,9},{9,10},{10,11},{11... | collective-permute-start | bytes 13832 | tf_op jit(solution)/shard_map/ppermute | solution.py:45
  40.1 24.1 %copy-start.10 = (bf16[2,256,16]{1,0,2:T(2,128)(2,1)S(1)}, bf16[2,256,16]{1,0,2:T(2,128)(2,1)}, u32[]{:S(2)}) copy-start(bf16[2,256,16]{1,0,2:T(2,128)(2,1)} %reshape.383) | copy-start | bytes 49156
  40.1 24.1 %copy-start.29 = (f32[12]{0:T(128)S(1)}, f32[12]{0:T(128)}, u32[]{:S(2)}) copy-start(f32[12]{0:T(128)} %get-tuple-element.494) | copy-start | bytes 148
  76.7 15.1 %copy-start.17 = (f32[384]{0:T(512)S(1)}, f32[384]{0:T(512)}, u32[]{:S(2)}) copy-start(f32[384]{0:T(512)} %get-tuple-element.383) | copy-start | bytes 4612
  79.3 11.7 %all-to-all-start.1 = ((bf16[8,2,32,384]{3,1,2,0:T(2,128)(2,1)}), bf16[8,2,32,384]{3,1,2,0:T(2,128)(2,1)S(1)}, u32[]{:S(2)}, u32[]{:S(2)}) async-start(bf16[8,2,32,384]{3,1,2,0:T(2,128)(2,1)} %bitcast_dynamic-update-slice_fusion.4), calls=%async_computation.1 | async-start | bytes 786432 | tf_op jit(solution)/shard_map/all_to_all | solution.py:12
  82.8 9.2 %copy-start.8 = (bf16[1,384,44]{1,0,2:T(2,128)(2,1)S(1)}, bf16[1,384,44]{1,0,2:T(2,128)(2,1)}, u32[]{:S(2)}) copy-start(bf16[1,384,44]{1,0,2:T(2,128)(2,1)} %get-tuple-element.473) | copy-start | bytes 101380
  94.6 7.2 %copy-start.12 = (f32[768]{0:T(1024)S(1)}, f32[768]{0:T(1024)}, u32[]{:S(2)}) copy-start(f32[768]{0:T(1024)} %get-tuple-element.371) | copy-start | bytes 9220
  94.6 7.2 %copy-start.13 = (f32[768]{0:T(1024)S(1)}, f32[768]{0:T(1024)}, u32[]{:S(2)}) copy-start(f32[768]{0:T(1024)} %get-tuple-element.372) | copy-start | bytes 9220
  94.7 7.2 %copy-start.14 = (f32[768]{0:T(1024)S(1)}, f32[768]{0:T(1024)}, u32[]{:S(2)}) copy-start(f32[768]{0:T(1024)} %get-tuple-element.373) | copy-start | bytes 9220
  95.7 5.2 %collective-permute-start.3 = (bf16[3,32]{0,1:T(8,128)(2,1)S(1)}, bf16[3,32]{0,1:T(8,128)(2,1)S(1)}, u32[]{:S(2)}, u32[]{:S(2)}) collective-permute-start(bf16[3,32]{0,1:T(8,128)(2,1)S(1)} %slice.398), channel_id=1, source_target_pairs={{0,1},{1,2},{2,3},{3,4},{4,5},{5,6},{6,7},{8,9},{9,10},{10,11},{11... | collective-permute-start | bytes 584 | tf_op jit(solution)/shard_map/ppermute | solution.py:45
  97.0 4.8 %collective-permute-start.2 = (bf16[3,768]{1,0:T(4,128)(2,1)S(1)}, bf16[3,768]{1,0:T(4,128)(2,1)S(1)}, u32[]{:S(2)}, u32[]{:S(2)}) collective-permute-start(bf16[3,768]{1,0:T(4,128)(2,1)S(1)} %slice.392), channel_id=1, source_target_pairs={{0,1},{1,2},{2,3},{3,4},{4,5},{5,6},{6,7},{8,9},{9,10},{10,11},{11... | collective-permute-start | bytes 13832 | tf_op jit(solution)/shard_map/ppermute | solution.py:45
  114.7 24.1 %copy-start.9 = (bf16[2,256,16]{1,0,2:T(2,128)(2,1)S(1)}, bf16[2,256,16]{1,0,2:T(2,128)(2,1)}, u32[]{:S(2)}) copy-start(bf16[2,256,16]{1,0,2:T(2,128)(2,1)} %reshape.392) | copy-start | bytes 49156
  114.7 24.1 %copy-start.27 = (f32[12]{0:T(128)S(1)}, f32[12]{0:T(128)}, u32[]{:S(2)}) copy-start(f32[12]{0:T(128)} %get-tuple-element.493) | copy-start | bytes 148
  (18 other events, 74.3 us)
